TPU v7x, 32 devices: a whole 2x2x4 slice. The times are simulated.
32 devices in a mesh: freq: 4 (over x, core), tile: 8 (over z, y).
Axes of the slice: x: 2, y: 2, z: 4, core: 2. Of those that a mesh axis runs over, the one named last changes fastest.
Arguments:
- plus_time: bfloat16 [128, 128, 12288], P('freq', None, 'tile'), may hold values from -6 to 6
- minus_time: bfloat16 [128, 128, 12288], P('freq', None, 'tile'), may hold values from -6 to 6
- gate_starts: int32 [128, 48], P('freq', 'tile'), may hold values from 0 to 64
- tile_ranks: int32 [4, 48, 48], P('freq', None, 'tile'), may hold values from 1 to 64, as said below
- u_factors: bfloat16 [4, 48, 48, 2, 64, 256], P('freq', 'tile'), may hold values from -0.109375 to 0.109375
- v_factors: bfloat16 [4, 48, 48, 2, 64, 256], P('freq', None, 'tile'), may hold values from -0.375 to 0.375
Outputs:
- minus_new: bfloat16 [4, 2, 128, 12288], P('freq', None, None, 'tile')
- plus_new: bfloat16 [4, 2, 128, 12288], P('freq', None, None, 'tile')
- cross_gram: float32 [4, 2, 128, 128], P('freq', None, 'tile')
- normal_gram: float32 [4, 2, 128, 128], P('freq', None, 'tile')
Inputs may be any that keep to these rules, and one draw needn't show every extreme that they name: `tile_ranks`: tiles with |i - j| <= 1 have rank 64; every other tile has rank at most 32, and some tile of every draw has exactly 32.
All inputs are finite; a program needn't handle non-finite values.
Results may differ from a plain program's by a relative error of at most 0.014.
Values may be sent and summed in bfloat16 or wider, within the bound.
A program may use at most 192 MiB of HBM per device.

v0:
```python
import math
import jax
import jax.numpy as jnp
from jax import lax
from jax.sharding import PartitionSpec as P

R = 12288
GATE = 64


def extended(x, sides, width):
    for axis, dim in sides:
        size, length = (lax.axis_size(axis), x.shape[dim])
        up = [(i, (i + 1) % size) for i in range(size - 1)]
        down = [(j, i) for i, j in up]
        last = lax.slice_in_dim(x, length - width, length, axis=dim)
        leading = lax.slice_in_dim(x, 0, width, axis=dim)
        before = lax.ppermute(last, axis, up)
        after = lax.ppermute(leading, axis, down)
        x = jnp.concatenate([before, x, after], axis=dim)
    return x


def make_table(freq_count, sample_count):
    freq_ids = lax.broadcasted_iota(jnp.int32, (freq_count, sample_count), 0)
    sample_ids = lax.broadcasted_iota(jnp.int32, (freq_count, sample_count), 1)
    phase_ids = freq_ids * sample_ids % sample_count
    angles = phase_ids.astype(jnp.float32) * (2.0 * math.pi / sample_count)
    amplitude = 1.0 / math.sqrt(GATE)
    return jnp.stack([jnp.cos(angles) * amplitude, -jnp.sin(angles) * amplitude]).astype(
        jnp.bfloat16
    )


def half_signs(entry_count):
    entry_ids = lax.broadcasted_iota(jnp.int32, (entry_count,), 0)
    return jnp.where(entry_ids < entry_count // 2, 1.0, -1.0).astype(jnp.float32)


def gate_field(traces, gate_starts):
    sources, samples, receivers = traces.shape
    blocks = gate_starts.shape[1]
    shaped = traces.reshape(sources, samples, blocks, receivers // blocks)
    sample_ids = lax.broadcasted_iota(jnp.int32, (1, samples, 1, 1), 1)
    starts = gate_starts[:, None, :, None]
    inside = (sample_ids >= starts) & (sample_ids < starts + GATE)
    kept = jnp.where(inside, shaped, jnp.zeros((), traces.dtype))
    return kept.reshape(sources, samples, receivers)


def on_device(plus_time, minus_time, gate_starts, tile_ranks, u_factors, v_factors):
    f_local = u_factors.shape[0]
    row_tiles = u_factors.shape[1]
    all_tiles = u_factors.shape[2]
    col_tiles = v_factors.shape[2]
    rank_depth = v_factors.shape[4]
    half_depth = rank_depth // 2
    freq_total = f_local * lax.axis_size("freq")
    sample_count = plus_time.shape[1]
    stacked = jnp.stack([gate_field(plus_time, gate_starts), gate_field(minus_time, gate_starts)])
    dft_table = make_table(freq_total, sample_count)
    local_spec = jnp.einsum(
        "cft,qstr->fcqsr", dft_table, stacked, preferred_element_type=jnp.float32
    ).astype(jnp.bfloat16)
    spectra = lax.all_to_all(local_spec, "freq", split_axis=0, concat_axis=3, tiled=True)
    both_sources = 2 * spectra.shape[3]
    columns = spectra.reshape(f_local, 2, both_sources, col_tiles, spectra.shape[4] // col_tiles)
    sign_vec = half_signs(both_sources)
    partial_c = jnp.einsum(
        "fijckr,fdsjr->fijcdks", v_factors, columns, preferred_element_type=jnp.float32
    )
    coeff_real = partial_c[:, :, :, 0, 0] - sign_vec * partial_c[:, :, :, 1, 1]
    coeff_imag = partial_c[:, :, :, 0, 1] + sign_vec * partial_c[:, :, :, 1, 0]
    rank_ids = lax.broadcasted_iota(jnp.int32, (1, 1, 1, rank_depth), 3)
    rank_mask = (rank_ids < tile_ranks[:, :, :, None]).astype(jnp.float32)[..., None]
    coeff_all = jnp.stack([coeff_real * rank_mask, coeff_imag * rank_mask], 3).astype(jnp.bfloat16)
    lower_part = coeff_all[:, :, :, :, :half_depth]
    lower_rows = lax.all_to_all(lower_part, "tile", split_axis=1, concat_axis=2, tiled=True)
    products = jnp.einsum(
        "fijckr,fijeks->fcesir",
        u_factors[:, :, :, :, :half_depth],
        lower_rows,
        preferred_element_type=jnp.float32,
    )
    block_start = lax.axis_index("tile") * col_tiles
    local_ids = lax.broadcasted_iota(jnp.int32, (col_tiles,), 0)
    global_cols = block_start + local_ids
    band_list = []
    for offset in (-1, 0, 1):
        band_rows = global_cols + offset
        valid = (band_rows >= 0) & (band_rows < all_tiles)
        clipped = jnp.clip(band_rows, 0, all_tiles - 1)
        picked = coeff_all[:, clipped, local_ids][:, :, :, half_depth:]
        band_list.append(
            jnp.where(valid[None, :, None, None, None], picked, jnp.zeros((), picked.dtype))
        )
    band_upper = jnp.stack(band_list, 1)
    padded_band = extended(band_upper, (("tile", 2),), 1)
    row_global = lax.axis_index("tile") * row_tiles + lax.broadcasted_iota(
        jnp.int32, (row_tiles,), 0
    )
    row_local = lax.broadcasted_iota(jnp.int32, (row_tiles,), 0)
    coeff_band = []
    u_band = []
    for position, offset in enumerate((-1, 0, 1)):
        coeff_band.append(padded_band[:, position, 1 - offset : 1 - offset + row_tiles])
        partner = jnp.clip(row_global - offset, 0, all_tiles - 1)
        u_band.append(u_factors[:, row_local, partner][:, :, :, half_depth:])
    band_products = jnp.einsum(
        "fdickr,fdieks->fcesir",
        jnp.stack(u_band, 1),
        jnp.stack(coeff_band, 1),
        preferred_element_type=jnp.float32,
    )
    products = products + band_products
    resp_real = products[:, 0, 0] - sign_vec[:, None, None] * products[:, 1, 1]
    resp_imag = products[:, 0, 1] + sign_vec[:, None, None] * products[:, 1, 0]
    response = jnp.stack([resp_real, resp_imag], 1).reshape(f_local, 2, both_sources, -1)
    rounded = response.astype(jnp.bfloat16)
    half_count = both_sources // 2
    minus_new = rounded[:, :, :half_count]
    plus_new = rounded[:, :, half_count:]
    gram_parts = jnp.einsum(
        "fczr,fesr->fczes", rounded, plus_new, preferred_element_type=jnp.float32
    )
    gram_real = gram_parts[:, 0, :, 0] + gram_parts[:, 1, :, 1]
    gram_imag = gram_parts[:, 1, :, 0] - gram_parts[:, 0, :, 1]
    row_ids = lax.broadcasted_iota(jnp.int32, (both_sources, 1), 0)
    row_scale = jnp.where(row_ids < half_count, 1.0 / math.sqrt(R), 1.0 / R).astype(jnp.float32)
    gram_all = jnp.stack([gram_real * row_scale, gram_imag * row_scale], 1)
    gram_all = gram_all.reshape(f_local, 2, 2, half_count, half_count).transpose(0, 2, 1, 3, 4)
    gram_total = lax.psum(gram_all.astype(jnp.bfloat16), "tile").astype(jnp.float32)
    row_share = half_count // lax.axis_size("tile")
    own_rows = lax.dynamic_slice_in_dim(
        gram_total, lax.axis_index("tile") * row_share, row_share, 3
    )
    return (minus_new, plus_new, own_rows[:, 0], own_rows[:, 1])


def solution(mesh):
    placed = (
        P("freq", None, "tile"),
        P("freq", None, "tile"),
        P("freq", "tile"),
        P("freq", None, "tile"),
        P("freq", "tile", None, None, None, None),
        P("freq", None, "tile", None, None, None),
    )
    return jax.shard_map(
        on_device,
        mesh=mesh,
        in_specs=placed,
        out_specs=(
            P("freq", None, None, "tile"),
            P("freq", None, None, "tile"),
            P("freq", None, "tile", None),
            P("freq", None, "tile", None),
        ),
        check_vma=False,
    )
```

profile of v0, /device:TPU:0, one launch (start us, length us, event | category | flops | bytes accessed | tf_op | source)
XLA Modules:
  0.0 496.3 jit_solution(5784172588843423811)
XLA Ops:
  7.2 0.7 broadcast_add_fusion
  7.9 0.8 copy.66
  8.8 0.1 fusion.50
  8.9 4.3 broadcast_in_dim.81
  13.2 14.4 %copy.68 = pred[32,128,1536]{2,1,0:T(8,128)(4,1)} copy(pred[32,128,1536]{1,2,0:T(8,128)(4,1)} %bitcast.187) | data formatting | bytes 12582912 | tf_op jit(solution)/shard_map/jit(_where)/broadcast_in_dim | solution.py:47
  27.6 15.3 %select_bitcast_fusion.1 = (bf16[1,32,128,1536]{3,2,1,0:T(8,128)(2,1)S(1)}, bf16[1,32,128,1536]{3,2,1,0:T(8,128)(2,1)}) fusion(pred[32,128,1536]{2,1,0:T(8,128)(4,1)} %copy.68, bf16[32,128,1536]{2,1,0:T(8,128)(2,1)} %param.6, bf16[32,128,1536]{2,1,0:T(8,128)(2,1)} %param.7), kind=kLoop, calls=%fused_computation.27 | loop fusion | flops 12582912 | bytes 56623104 | tf_op jit(solution)/shard_map/jit(_where)/select_n | solution.py:47
  42.9 6.8 %fusion.18 = bf16[4,2,2,32,1536]{4,0,1,3,2:T(4,128)(2,1)S(1)} fusion(bf16[1,32,128,1536]{3,2,1,0:T(8,128)(2,1)} %get-tuple-element.11, bf16[1,32,128,1536]{3,2,1,0:T(8,128)(2,1)S(1)} %get-tuple-element.10, bf16[1,4,128]{2,1,0:T(4,128)(2,1)S(1)} %get-tuple-element.24, bf16[1,4,128]{2,1,0:T(4,128)(2,1)S(1)} %get-tuple-element.25), kind=kOutput, calls=%fused_computation.37 | convolution fusion | flops 252448768 | bytes 26740736 | tf_op jit(solution)/shard_map/cft,qstr->fcqsr/dot_general | solution.py:62
  49.8 2.4 copy.70
  52.1 4.2 all-to-all-start
  56.4 0.1 fusion.49
  56.5 19.9 %all-to-all-done = bf16[4,2,2,32,1536]{4,1,3,2,0:T(2,128)(2,1)S(1)} async-done(((bf16[4,2,2,32,1536]{4,1,3,2,0:T(2,128)(2,1)}), bf16[4,2,2,32,1536]{4,1,3,2,0:T(2,128)(2,1)S(1)}, u32[]{:S(2)}, u32[]{:S(2)}) %all-to-all-start) | async-done | bytes 1572896 | tf_op jit(solution)/shard_map/all_to_all | solution.py:65
  76.4 1.4 copy.71
  77.8 3.3 reshape.598
  81.1 32.4 %convolution_bitcast_fusion = f32[1,48,6,2,2,64,256]{6,5,3,1,4,2,0:T(8,128)} fusion(bf16[2,256,6,256,1,1]{3,2,1,0,5,4:T(8,128)(2,1)S(1)} %bitcast.189, bf16[1,48,6,2,64,256]{5,4,3,2,1,0:T(8,128)(2,1)} %param.11), kind=kOutput, calls=%fused_computation.6 | convolution fusion | flops 9663676416 | bytes 95944704 | tf_op jit(solution)/shard_map/fijckr,fdsjr->fijcdks/dot_general | solution.py:69
  113.5 24.0 %fusion.12 = (bf16[1,48,6,1,64,256]{5,4,1,2,3,0:T(8,128)(2,1)S(1)}, bf16[1,48,6,1,64,256]{5,4,1,2,3,0:T(8,128)(2,1)S(1)}) fusion(f32[1,48,6,2,2,64,256]{6,5,3,1,4,2,0:T(8,128)} %convolution_bitcast_fusion, f32[48,6,64]{2,0,1:T(8,128)S(1)} %fusion.49, f32[256]{0:T(256)S(1)} %compare_select_fusion.4), kind=kLoop, calls=%fused_computation.29 | loop fusion | flops 37748736 | bytes 94446592 | tf_op jit(solution)/shard_map/stack | solution.py:76
  137.6 3.6 copy-done
  141.2 2.7 copy-done.1
  143.9 4.1 fusion.13
  148.0 9.0 %copy.77 = bf16[1,48,6,2,32,256]{5,4,2,3,0,1:T(8,128)(2,1)} copy(bf16[1,48,6,2,32,256]{5,4,1,2,3,0:T(8,128)(2,1)} %fusion.13) | data formatting | bytes 18874368 | tf_op jit(solution)/shard_map/slice | solution.py:77
  157.0 6.6 %all-to-all-start.1 = ((bf16[1,48,6,2,32,256]{5,4,2,3,0,1:T(8,128)(2,1)}), bf16[1,48,6,2,32,256]{5,4,2,3,0,1:T(8,128)(2,1)}, u32[]{:S(2)}, u32[]{:S(2)}) async-start(bf16[1,48,6,2,32,256]{5,4,2,3,0,1:T(8,128)(2,1)} %copy.77), calls=%async_computation.1 | async-start | bytes 18874368 | tf_op jit(solution)/shard_map/all_to_all | solution.py:78
  163.7 6.9 %gather_fusion.5 = bf16[6,2,64,256]{3,2,1,0:T(8,128)(2,1)S(1)} fusion(bf16[6,48,2,64,256]{4,3,2,1,0:T(8,128)(2,1)} %bitcast.205, s32[6]{0:T(128)S(1)} %get-tuple-element.28), kind=kCustom, calls=%fused_computation.5 | custom fusion | bytes 786480 | tf_op jit(solution)/shard_map/gather | solution.py:108
  170.7 6.9 %gather_fusion.4 = bf16[6,2,64,256]{3,2,1,0:T(8,128)(2,1)S(1)} fusion(bf16[6,48,2,64,256]{4,3,2,1,0:T(8,128)(2,1)} %bitcast.206, s32[6]{0:T(128)S(1)} %get-tuple-element.29), kind=kCustom, calls=%fused_computation.4 | custom fusion | bytes 786480 | tf_op jit(solution)/shard_map/gather | solution.py:108
  177.6 6.9 %gather_fusion.3 = bf16[6,2,64,256]{3,2,1,0:T(8,128)(2,1)S(1)} fusion(bf16[6,48,2,64,256]{4,3,2,1,0:T(8,128)(2,1)} %bitcast.207, s32[6]{0:T(128)S(1)} %get-tuple-element.30), kind=kCustom, calls=%fused_computation.3 | custom fusion | bytes 786480 | tf_op jit(solution)/shard_map/gather | solution.py:108
  184.7 16.5 %fusion.1 = bf16[48,6,2,64,256]{4,3,0,1,2:T(8,128)(2,1)} fusion(bf16[1,48,6,1,64,256]{5,4,1,2,3,0:T(8,128)(2,1)} %copy-done, bf16[1,48,6,1,64,256]{5,4,1,2,3,0:T(8,128)(2,1)} %copy-done.1), kind=kLoop, calls=%fused_computation.12 | loop fusion | flops 9437184 | bytes 37748736 | tf_op jit(solution)/shard_map/stack | solution.py:76
  201.2 6.9 %gather_fusion.2 = bf16[6,2,64,256]{3,2,1,0:T(8,128)(2,1)S(1)} fusion(bf16[48,6,2,64,256]{4,3,0,1,2:T(8,128)(2,1)} %fusion.1, s32[6]{0:T(128)S(1)} %get-tuple-element.31), kind=kCustom, calls=%fused_computation.2 | custom fusion | bytes 786480 | tf_op jit(solution)/shard_map/gather | solution.py:93
  208.2 6.9 %gather_fusion.1 = bf16[6,2,64,256]{3,2,1,0:T(8,128)(2,1)S(1)} fusion(bf16[48,6,2,64,256]{4,3,0,1,2:T(8,128)(2,1)} %fusion.1, s32[6]{0:T(128)S(1)} %get-tuple-element.32), kind=kCustom, calls=%fused_computation.1 | custom fusion | bytes 786480 | tf_op jit(solution)/shard_map/gather | solution.py:93
  215.1 6.9 %gather_fusion = bf16[6,2,64,256]{3,2,1,0:T(8,128)(2,1)S(1)} fusion(bf16[48,6,2,64,256]{4,3,0,1,2:T(8,128)(2,1)} %fusion.1, s32[6]{0:T(128)S(1)} %get-tuple-element.33), kind=kCustom, calls=%fused_computation | custom fusion | bytes 786480 | tf_op jit(solution)/shard_map/gather | solution.py:93
  222.2 0.1 fusion.47
  222.5 1.3 collective-permute-start
  223.8 4.6 collective-permute-start.1
  228.3 141.7 %all-to-all-done.1 = bf16[1,48,6,2,32,256]{5,4,2,3,0,1:T(8,128)(2,1)} async-done(((bf16[1,48,6,2,32,256]{5,4,2,3,0,1:T(8,128)(2,1)}), bf16[1,48,6,2,32,256]{5,4,2,3,0,1:T(8,128)(2,1)}, u32[]{:S(2)}, u32[]{:S(2)}) %all-to-all-start.1) | async-done | bytes 9437216 | tf_op jit(solution)/shard_map/all_to_all | solution.py:78
  370.0 9.1 %copy.78 = bf16[1,48,6,2,32,256]{5,4,3,2,1,0:T(8,128)(2,1)} copy(bf16[1,48,6,2,32,256]{5,4,2,3,0,1:T(8,128)(2,1)} %all-to-all-done.1) | data formatting | bytes 18874368 | tf_op jit(solution)/shard_map/all_to_all | solution.py:78
  379.1 9.5 %copy.79 = bf16[1,6,8,6,2,32,256]{6,5,4,3,2,1,0:T(8,128)(2,1)} copy(bf16[1,6,8,6,2,32,256]{6,5,4,3,1,2,0:T(8,128)(2,1)} %bitcast.186) | data formatting | bytes 18874368 | tf_op jit(solution)/shard_map/all_to_all | solution.py:78
  388.6 12.0 %fusion.14 = f32[6,2,256,2,256,1]{2,4,5,3,1,0:T(8,128)} fusion(bf16[6,48,2,32,256,1]{4,3,2,1,0,5:T(8,128)(2,1)} %bitcast.188, bf16[1,6,48,2,64,256]{5,4,3,2,1,0:T(8,128)(2,1)} %param.10), kind=kOutput, calls=%fused_computation.32 | convolution fusion | flops 4831838208 | bytes 25165824 | tf_op jit(solution)/shard_map/fijckr,fijeks->fcesir/dot_general | solution.py:79
  400.6 3.5 fusion.16
  404.2 2.2 fusion.64
  406.4 3.0 copy.83
  409.4 3.0 copy.84
  412.5 1.6 copy.85
  414.1 0.5 copy.86
  414.6 3.1 add_convert_fusion
  417.7 1.0 pad_maximum_fusion.1
  418.7 0.6 fusion.23
  419.4 0.1 multiply_convert_fusion.1
  419.5 0.7 maximum_bitcast_fusion.12
  420.2 68.0 %all-reduce.2.cloned.1.call-done = bf16[1,2,2,128,128]{4,3,2,1,0:T(8,128)(2,1)} async-done(((bf16[1,2,2,128,128]{4,3,2,1,0:T(8,128)(2,1)}), bf16[1,2,2,128,128]{4,3,2,1,0:T(8,128)(2,1)}) %all-reduce.2.cloned.1.call-update) | async-done | bytes 131088 | tf_op jit(solution)/shard_map/psum | solution.py:132
  488.1 0.7 dynamic-slice_convert_fusion
  488.9 0.6 slice_bitcast_fusion.7
  (28 shorter events, 0.6 us)
Async XLA Ops:
  49.7 6.6 %copy-start.3 = (s32[1,48,6]{1,0,2:T(1,128)S(1)}, s32[1,48,6]{1,0,2:T(1,128)}, u32[]{:S(2)}) copy-start(s32[1,48,6]{1,0,2:T(1,128)} %param.9) | copy-start | bytes 3460
  52.1 24.3 %all-to-all-start = ((bf16[4,2,2,32,1536]{4,1,3,2,0:T(2,128)(2,1)}), bf16[4,2,2,32,1536]{4,1,3,2,0:T(2,128)(2,1)S(1)}, u32[]{:S(2)}, u32[]{:S(2)}) async-start(bf16[4,2,2,32,1536]{4,1,3,2,0:T(2,128)(2,1)} %copy.70), calls=%async_computation | async-start | bytes 3145728 | tf_op jit(solution)/shard_map/all_to_all | solution.py:65
  137.6 3.6 copy-start
  137.6 6.4 %copy-start.1 = (bf16[1,48,6,1,64,256]{5,4,1,2,3,0:T(8,128)(2,1)}, bf16[1,48,6,1,64,256]{5,4,1,2,3,0:T(8,128)(2,1)S(1)}, u32[]{:S(2)}) copy-start(bf16[1,48,6,1,64,256]{5,4,1,2,3,0:T(8,128)(2,1)S(1)} %get-tuple-element.5) | copy-start | bytes 28311556
  157.0 213.0 %all-to-all-start.1 = ((bf16[1,48,6,2,32,256]{5,4,2,3,0,1:T(8,128)(2,1)}), bf16[1,48,6,2,32,256]{5,4,2,3,0,1:T(8,128)(2,1)}, u32[]{:S(2)}, u32[]{:S(2)}) async-start(bf16[1,48,6,2,32,256]{5,4,2,3,0,1:T(8,128)(2,1)} %copy.77), calls=%async_computation.1 | async-start | bytes 18874368 | tf_op jit(solution)/shard_map/all_to_all | solution.py:78
  163.6 324.5 %all-reduce.2.cloned.1.call-start = ((), (), s32[]{:S(2)}) async-start(), calls=%async_computation.2 | async-start | bytes 262144 | tf_op jit(solution)/shard_map/psum | solution.py:132
  222.5 178.2 %collective-permute-start = (bf16[1,3,1,2,32,256]{5,4,3,2,1,0:T(8,128)(2,1)S(1)}, bf16[1,3,1,2,32,256]{5,4,3,2,1,0:T(8,128)(2,1)S(1)}, u32[]{:S(2)}, u32[]{:S(2)}) collective-permute-start(bf16[1,3,1,2,32,256]{5,4,3,2,1,0:T(8,128)(2,1)S(1)} %get-tuple-element.14), channel_id=1, source_target_pairs={{1,0},{2,1},{3,2},{4,3},{5,4},{6,5},{7,6},{9,8},{10,9},{11,10},{12... | collective-permute-start | bytes 294920 | tf_op jit(solution)/shard_map/ppermute | solution.py:19
  223.8 176.9 %collective-permute-start.1 = (bf16[1,3,1,2,32,256]{5,4,3,2,1,0:T(8,128)(2,1)S(1)}, bf16[1,3,1,2,32,256]{5,4,3,2,1,0:T(8,128)(2,1)S(1)}, u32[]{:S(2)}, u32[]{:S(2)}) collective-permute-start(bf16[1,3,1,2,32,256]{5,4,3,2,1,0:T(8,128)(2,1)S(1)} %get-tuple-element.15), channel_id=1, source_target_pairs={{0,1},{1,2},{2,3},{3,4},{4,5},{5,6},{6,7},{8,9},{9,10},{10,11},{11... | collective-permute-start | bytes 294920 | tf_op jit(solution)/shard_map/ppermute | solution.py:18
  418.7 70.7 %copy-start.2 = (bf16[1,2,128,1536]{3,2,1,0:T(8,128)(2,1)}, bf16[1,2,128,1536]{3,2,1,0:T(8,128)(2,1)S(1)}, u32[]{:S(2)}) copy-start(bf16[1,2,128,1536]{3,2,1,0:T(8,128)(2,1)S(1)} %get-tuple-element.12) | copy-start | bytes 2359300
Sparse Core Ops, SparseCore 0:
  420.3 67.7 all-reduce.1
where the time goes:
time: 498 us; the launch traced here: 496 us
  waiting for transfers between devices  230 us (46%)
  local copies, waits for them, and re-layouts  113 us (23%)
  other arithmetic  67 us (13%)
  matrix products  55.3 us (11%)
  starting transfers between devices  16.7 us (3%)
  between operations  14.3 us (3%)
    all_to_all x1, waiting for transfers between devices, on_device(): lax.all_to_all(lower_part, 'tile', split_axis=1, concat_axis=2, tiled=True)  142 us
    psum x1, waiting for transfers between devices, on_device(): lax.psum(gram_all.astype(jnp.bfloat16), 'tile').astype(jnp.float32)  68 us
    another operation x3, other arithmetic, on_device(): jnp.stack([coeff_real * rank_mask, coeff_imag * rank_mask], 3)  44.6 us
    dot_general x1, matrix products, on_device(): jnp.einsum('fijckr,fdsjr->fijcdks', v_factors, columns, preferred_element...  32.4 us
    gather x3, local copies, waits for them, and re-layouts, on_device(): u_band.append(u_factors[:, row_local, partner][:, :, :, half_depth:])  20.8 us
    gather x3, local copies, waits for them, and re-layouts, on_device(): picked = coeff_all[:, clipped, local_ids][:, :, :, half_depth:]  20.8 us
    all_to_all x1, waiting for transfers between devices, on_device(): lax.all_to_all(local_spec, 'freq', split_axis=0, concat_axis=3, tiled=True)  19.9 us
    broadcast_in_dim x2, local copies, waits for them, and re-layouts, gate_field(): kept = jnp.where(inside, shaped, jnp.zeros((), traces.dtype))  18.7 us
  transfers between devices with their start and end apart: 5, of which 3 were waited for; matrix products, arithmetic and copies ran while one was open for 18% of the time, Pallas kernels for 0%

commit v1 on v0

--- a/solution.py
+++ b/solution.py
@@ -75,7 +75,12 @@
     rank_mask = (rank_ids < tile_ranks[:, :, :, None]).astype(jnp.float32)[..., None]
     coeff_all = jnp.stack([coeff_real * rank_mask, coeff_imag * rank_mask], 3).astype(jnp.bfloat16)
     lower_part = coeff_all[:, :, :, :, :half_depth]
-    lower_rows = lax.all_to_all(lower_part, "tile", split_axis=1, concat_axis=2, tiled=True)
+    lower_rows = jnp.concatenate(
+        lax.all_to_all(
+            jnp.stack(jnp.split(lower_part, lax.axis_size("tile"), axis=1)), "tile", 0, 0
+        ),
+        axis=2,
+    )
     products = jnp.einsum(
         "fijckr,fijeks->fcesir",
         u_factors[:, :, :, :, :half_depth],

time: 498 us -> 480 us (0.964)
  local copies, waits for them, and re-layouts: 113 us -> 88.5 us
  other arithmetic: 67 us -> 74.6 us
    all_to_all x2 -> x0, local copies, waits for them, and re-layouts: 18.6 us -> none  [on_device(): lax.all_to_all(lower_part, 'tile', split_axis=1, concat_axis=2, tiled=True)]
    unnamed x0 -> x7, other arithmetic: none -> 10.7 us
    reshape x0 -> x1, local copies, waits for them, and re-layouts: none -> 9.02 us  [on_device(): jnp.concatenate(lax.all_to_all(jnp.stack(jnp.split(lower_part, lax.axis_s...]
    slice x1 -> x0, local copies, waits for them, and re-layouts: 9 us -> none  [on_device(): lower_part = coeff_all[:, :, :, :, :half_depth]]
    unnamed x10, local copies, waits for them, and re-layouts: 7.14 us -> 0.79 us
    another operation x3 -> x2, other arithmetic: 44.6 us -> 40.5 us  [on_device(): jnp.stack([coeff_real * rank_mask, coeff_imag * rank_mask], 3)]
  transfers between devices with their start and end apart: 5 -> 5, of which waited for: 3 -> 3; matrix products, arithmetic and copies ran while one was open for 18% -> 17% of each run, Pallas kernels for 0% -> 0%
where the time goes in v1:
time: 480 us; the launch traced here: 479 us
  waiting for transfers between devices  229 us (48%)
  local copies, waits for them, and re-layouts  88.5 us (18%)
  other arithmetic  74.6 us (16%)
  matrix products  55.4 us (12%)
  starting transfers between devices  16.9 us (4%)
  between operations  14.3 us (3%)
    all_to_all x1, waiting for transfers between devices, on_device(): lax.all_to_all(jnp.stack(jnp.split(lower_part, lax.axis_size('tile'), axi...  142 us
    psum x1, waiting for transfers between devices, on_device(): lax.psum(gram_all.astype(jnp.bfloat16), 'tile').astype(jnp.float32)  67.9 us
    another operation x2, other arithmetic, on_device(): jnp.stack([coeff_real * rank_mask, coeff_imag * rank_mask], 3)  40.5 us
    dot_general x1, matrix products, on_device(): jnp.einsum('fijckr,fdsjr->fijcdks', v_factors, columns, preferred_element...  32.4 us
    gather x3, local copies, waits for them, and re-layouts, on_device(): u_band.append(u_factors[:, row_local, partner][:, :, :, half_depth:])  20.8 us
    gather x3, local copies, waits for them, and re-layouts, on_device(): picked = coeff_all[:, clipped, local_ids][:, :, :, half_depth:]  20.8 us
    all_to_all x1, waiting for transfers between devices, on_device(): lax.all_to_all(local_spec, 'freq', split_axis=0, concat_axis=3, tiled=True)  19.9 us
    broadcast_in_dim x2, local copies, waits for them, and re-layouts, gate_field(): kept = jnp.where(inside, shaped, jnp.zeros((), traces.dtype))  18.7 us
  transfers between devices with their start and end apart: 5, of which 3 were waited for; matrix products, arithmetic and copies ran while one was open for 17% of the time, Pallas kernels for 0%

profile of v1, /device:TPU:0, one launch (start us, length us, event | category | flops | bytes accessed | tf_op | source)
XLA Modules:
  0.0 479.1 jit_solution(6255236589496641835)
XLA Ops:
  7.2 0.7 broadcast_add_fusion
  7.9 0.8 copy.44
  8.9 4.3 broadcast_in_dim.81
  13.2 14.4 %copy.46 = pred[32,128,1536]{2,1,0:T(8,128)(4,1)} copy(pred[32,128,1536]{1,2,0:T(8,128)(4,1)} %bitcast.200) | data formatting | bytes 12582912 | tf_op jit(solution)/shard_map/jit(_where)/broadcast_in_dim | solution.py:47
  27.6 15.3 %select_bitcast_fusion.1 = (bf16[1,32,128,1536]{3,2,1,0:T(8,128)(2,1)S(1)}, bf16[1,32,128,1536]{3,2,1,0:T(8,128)(2,1)}) fusion(pred[32,128,1536]{2,1,0:T(8,128)(4,1)} %copy.46, bf16[32,128,1536]{2,1,0:T(8,128)(2,1)} %param.6, bf16[32,128,1536]{2,1,0:T(8,128)(2,1)} %param.7), kind=kLoop, calls=%fused_computation.41 | loop fusion | flops 12582912 | bytes 56623104 | tf_op jit(solution)/shard_map/jit(_where)/select_n | solution.py:47
  42.9 6.8 %fusion.17 = bf16[4,2,2,32,1536]{4,0,1,3,2:T(4,128)(2,1)S(1)} fusion(bf16[1,32,128,1536]{3,2,1,0:T(8,128)(2,1)} %get-tuple-element.11, bf16[1,32,128,1536]{3,2,1,0:T(8,128)(2,1)S(1)} %get-tuple-element.10, bf16[1,4,128]{2,1,0:T(4,128)(2,1)S(1)} %get-tuple-element.24, bf16[1,4,128]{2,1,0:T(4,128)(2,1)S(1)} %get-tuple-element.25), kind=kOutput, calls=%fused_computation.50 | convolution fusion | flops 252448768 | bytes 26740736 | tf_op jit(solution)/shard_map/cft,qstr->fcqsr/dot_general | solution.py:62
  49.8 2.4 copy.48
  52.1 4.2 all-to-all-start
  56.5 19.9 %all-to-all-done = bf16[4,2,2,32,1536]{4,1,3,2,0:T(2,128)(2,1)S(1)} async-done(((bf16[4,2,2,32,1536]{4,1,3,2,0:T(2,128)(2,1)}), bf16[4,2,2,32,1536]{4,1,3,2,0:T(2,128)(2,1)S(1)}, u32[]{:S(2)}, u32[]{:S(2)}) %all-to-all-start) | async-done | bytes 1572896 | tf_op jit(solution)/shard_map/all_to_all | solution.py:65
  76.4 1.4 copy.49
  77.8 3.3 reshape.602
  81.1 32.4 %convolution_bitcast_fusion = f32[1,48,6,2,2,64,256]{6,5,3,1,4,2,0:T(8,128)} fusion(bf16[2,256,6,256,1,1]{3,2,1,0,5,4:T(8,128)(2,1)S(1)} %bitcast.202, bf16[1,48,6,2,64,256]{5,4,3,2,1,0:T(8,128)(2,1)} %param.11), kind=kOutput, calls=%fused_computation.23 | convolution fusion | flops 9663676416 | bytes 95944704 | tf_op jit(solution)/shard_map/fijckr,fdsjr->fijcdks/dot_general | solution.py:69
  113.5 24.0 %fusion.11 = (bf16[1,48,6,1,64,256]{5,4,1,2,3,0:T(8,128)(2,1)S(1)}, bf16[1,48,6,1,64,256]{5,4,1,2,3,0:T(8,128)(2,1)S(1)}) fusion(f32[1,48,6,2,2,64,256]{6,5,3,1,4,2,0:T(8,128)} %convolution_bitcast_fusion, f32[48,6,64]{2,0,1:T(8,128)S(1)} %fusion.56, f32[256]{0:T(256)S(1)} %compare_select_fusion.4), kind=kLoop, calls=%fused_computation.42 | loop fusion | flops 37748736 | bytes 94446592 | tf_op jit(solution)/shard_map/stack | solution.py:76
  137.6 1.2 bitcast_dynamic-update-slice_fusion.7
  138.8 1.5 bitcast_dynamic-update-slice_fusion.6
  140.3 1.7 bitcast_dynamic-update-slice_fusion.5
  142.1 2.0 bitcast_dynamic-update-slice_fusion.4
  144.1 1.9 bitcast_dynamic-update-slice_fusion.3
  146.0 1.2 bitcast_dynamic-update-slice_fusion.2
  147.1 1.1 bitcast_dynamic-update-slice_fusion.1
  148.2 1.1 bitcast_dynamic-update-slice_fusion
  149.3 6.6 %all-to-all-start.1 = ((bf16[8,1,6,6,2,32,256]{6,5,2,3,4,1,0:T(8,128)(2,1)}), bf16[8,1,6,6,2,32,256]{6,5,2,3,4,1,0:T(8,128)(2,1)}, u32[]{:S(2)}, u32[]{:S(2)}) async-start(bf16[8,1,6,6,2,32,256]{6,5,2,3,4,1,0:T(8,128)(2,1)} %bitcast_dynamic-update-slice_fusion), calls=%async_computation.1 | async-start | bytes 18874368 | tf_op jit(solution)/shard_map/all_to_all | solution.py:79
  156.0 0.2 all-reduce.2.cloned.1.call-start
  156.2 6.9 %gather_fusion.5 = bf16[6,2,64,256]{3,2,1,0:T(8,128)(2,1)S(1)} fusion(bf16[6,48,2,64,256]{4,3,2,1,0:T(8,128)(2,1)} %bitcast.218, s32[6]{0:T(128)S(1)} %get-tuple-element.28), kind=kCustom, calls=%fused_computation.5 | custom fusion | bytes 786480 | tf_op jit(solution)/shard_map/gather | solution.py:113
  163.2 6.9 %gather_fusion.4 = bf16[6,2,64,256]{3,2,1,0:T(8,128)(2,1)S(1)} fusion(bf16[6,48,2,64,256]{4,3,2,1,0:T(8,128)(2,1)} %bitcast.219, s32[6]{0:T(128)S(1)} %get-tuple-element.29), kind=kCustom, calls=%fused_computation.4 | custom fusion | bytes 786480 | tf_op jit(solution)/shard_map/gather | solution.py:113
  170.1 6.9 %gather_fusion.3 = bf16[6,2,64,256]{3,2,1,0:T(8,128)(2,1)S(1)} fusion(bf16[6,48,2,64,256]{4,3,2,1,0:T(8,128)(2,1)} %bitcast.220, s32[6]{0:T(128)S(1)} %get-tuple-element.30), kind=kCustom, calls=%fused_computation.3 | custom fusion | bytes 786480 | tf_op jit(solution)/shard_map/gather | solution.py:113
  177.2 16.5 %fusion.1 = bf16[48,6,2,64,256]{4,3,0,1,2:T(8,128)(2,1)} fusion(bf16[1,48,6,1,64,256]{5,4,1,2,3,0:T(8,128)(2,1)} %copy-done.1, bf16[1,48,6,1,64,256]{5,4,1,2,3,0:T(8,128)(2,1)} %copy-done), kind=kLoop, calls=%fused_computation.26 | loop fusion | flops 9437184 | bytes 37748736 | tf_op jit(solution)/shard_map/stack | solution.py:76
  193.7 6.9 %gather_fusion.2 = bf16[6,2,64,256]{3,2,1,0:T(8,128)(2,1)S(1)} fusion(bf16[48,6,2,64,256]{4,3,0,1,2:T(8,128)(2,1)} %fusion.1, s32[6]{0:T(128)S(1)} %get-tuple-element.31), kind=kCustom, calls=%fused_computation.2 | custom fusion | bytes 786480 | tf_op jit(solution)/shard_map/gather | solution.py:98
  200.7 6.9 %gather_fusion.1 = bf16[6,2,64,256]{3,2,1,0:T(8,128)(2,1)S(1)} fusion(bf16[48,6,2,64,256]{4,3,0,1,2:T(8,128)(2,1)} %fusion.1, s32[6]{0:T(128)S(1)} %get-tuple-element.32), kind=kCustom, calls=%fused_computation.1 | custom fusion | bytes 786480 | tf_op jit(solution)/shard_map/gather | solution.py:98
  207.6 6.9 %gather_fusion = bf16[6,2,64,256]{3,2,1,0:T(8,128)(2,1)S(1)} fusion(bf16[48,6,2,64,256]{4,3,0,1,2:T(8,128)(2,1)} %fusion.1, s32[6]{0:T(128)S(1)} %get-tuple-element.33), kind=kCustom, calls=%fused_computation | custom fusion | bytes 786480 | tf_op jit(solution)/shard_map/gather | solution.py:98
  215.0 1.3 collective-permute-start
  216.3 4.6 collective-permute-start.1
  220.8 141.5 %all-to-all-done.1 = bf16[8,1,6,6,2,32,256]{6,5,2,3,4,1,0:T(8,128)(2,1)} async-done(((bf16[8,1,6,6,2,32,256]{6,5,2,3,4,1,0:T(8,128)(2,1)}), bf16[8,1,6,6,2,32,256]{6,5,2,3,4,1,0:T(8,128)(2,1)}, u32[]{:S(2)}, u32[]{:S(2)}) %all-to-all-start.1) | async-done | bytes 9437216 | tf_op jit(solution)/shard_map/all_to_all | solution.py:79
  362.3 9.0 %copy.55 = bf16[1,6,8,6,2,32,256]{6,5,4,3,2,1,0:T(8,128)(2,1)} copy(bf16[1,6,8,6,2,32,256]{6,5,1,3,4,0,2:T(8,128)(2,1)} %bitcast.30) | data formatting | bytes 18874368 | tf_op jit(solution)/shard_map/reshape | solution.py:78
  371.4 12.0 %fusion.13 = f32[6,2,256,2,256,1]{2,4,5,3,1,0:T(8,128)} fusion(bf16[6,48,2,32,256,1]{4,3,2,1,0,5:T(8,128)(2,1)} %bitcast.201, bf16[1,6,48,2,64,256]{5,4,3,2,1,0:T(8,128)(2,1)} %param.10), kind=kOutput, calls=%fused_computation.45 | convolution fusion | flops 4831838208 | bytes 25165824 | tf_op jit(solution)/shard_map/fijckr,fijeks->fcesir/dot_general | solution.py:84
  383.4 3.5 fusion.15
  386.9 2.2 fusion.71
  389.2 3.0 copy.59
  392.2 3.0 copy.60
  395.2 1.6 copy.61
  396.9 0.5 copy.62
  397.3 3.1 add_convert_fusion
  400.5 1.0 pad_maximum_fusion.1
  401.5 0.6 fusion.22
  402.3 0.7 maximum_bitcast_fusion.12
  403.0 67.9 %all-reduce.2.cloned.1.call-done = bf16[1,2,2,128,128]{4,3,2,1,0:T(8,128)(2,1)} async-done(((bf16[1,2,2,128,128]{4,3,2,1,0:T(8,128)(2,1)}), bf16[1,2,2,128,128]{4,3,2,1,0:T(8,128)(2,1)}) %all-reduce.2.cloned.1.call-update) | async-done | bytes 131088 | tf_op jit(solution)/shard_map/psum | solution.py:137
  470.9 0.7 dynamic-slice_convert_fusion
  471.6 0.6 slice_bitcast_fusion.7
  (33 shorter events, 1.0 us)
Async XLA Ops:
  49.7 6.6 %copy-start.3 = (s32[1,48,6]{1,0,2:T(1,128)S(1)}, s32[1,48,6]{1,0,2:T(1,128)}, u32[]{:S(2)}) copy-start(s32[1,48,6]{1,0,2:T(1,128)} %param.9) | copy-start | bytes 3460
  52.1 24.3 %all-to-all-start = ((bf16[4,2,2,32,1536]{4,1,3,2,0:T(2,128)(2,1)}), bf16[4,2,2,32,1536]{4,1,3,2,0:T(2,128)(2,1)S(1)}, u32[]{:S(2)}, u32[]{:S(2)}) async-start(bf16[4,2,2,32,1536]{4,1,3,2,0:T(2,128)(2,1)} %copy.48), calls=%async_computation | async-start | bytes 3145728 | tf_op jit(solution)/shard_map/all_to_all | solution.py:65
  137.6 10.7 %copy-start = (bf16[1,48,6,1,64,256]{5,4,1,2,3,0:T(8,128)(2,1)}, bf16[1,48,6,1,64,256]{5,4,1,2,3,0:T(8,128)(2,1)S(1)}, u32[]{:S(2)}) copy-start(bf16[1,48,6,1,64,256]{5,4,1,2,3,0:T(8,128)(2,1)S(1)} %get-tuple-element.4) | copy-start | bytes 28311556
  137.6 10.7 %copy-start.1 = (bf16[1,48,6,1,64,256]{5,4,1,2,3,0:T(8,128)(2,1)}, bf16[1,48,6,1,64,256]{5,4,1,2,3,0:T(8,128)(2,1)S(1)}, u32[]{:S(2)}) copy-start(bf16[1,48,6,1,64,256]{5,4,1,2,3,0:T(8,128)(2,1)S(1)} %get-tuple-element.5) | copy-start | bytes 28311556
  149.3 213.0 %all-to-all-start.1 = ((bf16[8,1,6,6,2,32,256]{6,5,2,3,4,1,0:T(8,128)(2,1)}), bf16[8,1,6,6,2,32,256]{6,5,2,3,4,1,0:T(8,128)(2,1)}, u32[]{:S(2)}, u32[]{:S(2)}) async-start(bf16[8,1,6,6,2,32,256]{6,5,2,3,4,1,0:T(8,128)(2,1)} %bitcast_dynamic-update-slice_fusion), calls=%async_computation.1 | async-start | bytes 18874368 | tf_op jit(solution)/shard_map/all_to_all | solution.py:79
  156.0 315.0 %all-reduce.2.cloned.1.call-start = ((), (), s32[]{:S(2)}) async-start(), calls=%async_computation.2 | async-start | bytes 262144 | tf_op jit(solution)/shard_map/psum | solution.py:137
  215.0 168.4 %collective-permute-start = (bf16[1,3,1,2,32,256]{5,4,3,2,1,0:T(8,128)(2,1)S(1)}, bf16[1,3,1,2,32,256]{5,4,3,2,1,0:T(8,128)(2,1)S(1)}, u32[]{:S(2)}, u32[]{:S(2)}) collective-permute-start(bf16[1,3,1,2,32,256]{5,4,3,2,1,0:T(8,128)(2,1)S(1)} %get-tuple-element.14), channel_id=1, source_target_pairs={{1,0},{2,1},{3,2},{4,3},{5,4},{6,5},{7,6},{9,8},{10,9},{11,10},{12... | collective-permute-start | bytes 294920 | tf_op jit(solution)/shard_map/ppermute | solution.py:19
  216.3 167.1 %collective-permute-start.1 = (bf16[1,3,1,2,32,256]{5,4,3,2,1,0:T(8,128)(2,1)S(1)}, bf16[1,3,1,2,32,256]{5,4,3,2,1,0:T(8,128)(2,1)S(1)}, u32[]{:S(2)}, u32[]{:S(2)}) collective-permute-start(bf16[1,3,1,2,32,256]{5,4,3,2,1,0:T(8,128)(2,1)S(1)} %get-tuple-element.15), channel_id=1, source_target_pairs={{0,1},{1,2},{2,3},{3,4},{4,5},{5,6},{6,7},{8,9},{9,10},{10,11},{11... | collective-permute-start | bytes 294920 | tf_op jit(solution)/shard_map/ppermute | solution.py:18
  401.5 70.7 %copy-start.2 = (bf16[1,2,128,1536]{3,2,1,0:T(8,128)(2,1)}, bf16[1,2,128,1536]{3,2,1,0:T(8,128)(2,1)S(1)}, u32[]{:S(2)}) copy-start(bf16[1,2,128,1536]{3,2,1,0:T(8,128)(2,1)S(1)} %get-tuple-element.12) | copy-start | bytes 2359300
Sparse Core Ops, SparseCore 0:
  403.1 67.7 all-reduce.1
